TPU v7x, 256 devices: a whole 4x4x8 slice. The times are simulated.
256 devices in a mesh: row: 8 (over z), col: 32 (over y, x, core).
Axes of the slice: x: 4, y: 4, z: 8, core: 2. Of those that a mesh axis runs over, the one named last changes fastest.
Arguments:
- factor: bfloat16 [32, 8, 8, 32, 128, 128], P(None, 'row', None, 'col'), may hold values from -0.046875 to 0.046875
- pattern: int32 [32, 8, 8, 32], P(None, 'row', None, 'col'), may hold values 0 or 1
- loads: float32 [8, 32, 128, 256], P(None, 'col'), may hold values from -6 to 6
- block_inverse: float32 [8, 32, 128, 128], P(None, 'col'), may hold values from -1 to 2, as said below
Outputs:
- solution: float32 [8, 32, 128, 256], P(None, 'col')
Inputs may be any that keep to these rules, and one draw needn't show every extreme that they name: `block_inverse`: each block is lower triangular with diagonal entries between 0.5 and 1.5.
All inputs are finite; a program needn't handle non-finite values. No bound on the sum of `pattern` on one device may be relied on, other than what follows from the above.
Results may differ from a plain program's by a relative error of at most 0.0045.
Values may be sent and summed in bfloat16 or wider, within the bound.
No kernel may reach another device: no remote copies, remote signals or barrier semaphores. Data moves between devices by JAX's collectives and lax.ppermute only.
A program may use at most 128 MiB of HBM per device.

v0:
```python
import jax
import jax.numpy as jnp
from jax import lax
from jax.sharding import PartitionSpec as P

LEVELS = 8


def spread(value, axis, source):
    kept = jnp.where(lax.axis_index(axis) == source, value, 0).astype(value.dtype)
    return lax.psum(kept, axis)


def per_device(factor, pattern, loads, block_inverse):
    row_count = lax.axis_size("row")
    col_count = lax.axis_size("col")
    groups = col_count // row_count
    my_row = lax.axis_index("row")
    my_col = lax.axis_index("col")
    masked = factor[:, 0, :, 0] * pattern[:, 0, :, 0].astype(jnp.bfloat16)[:, :, None, None]
    per_row = factor.shape[0] // LEVELS
    per_col = factor.shape[2] // LEVELS
    rhs_local = loads[:, 0]
    inverse_local = block_inverse[:, 0]
    forward_vals = []
    forward_low = []
    for level_id in range(LEVELS):
        rhs_level = rhs_local[level_id * per_col : (level_id + 1) * per_col]
        inverse_level = inverse_local[level_id * per_col : (level_id + 1) * per_col]
        if level_id > 0:
            panel = masked[level_id * per_row : (level_id + 1) * per_row, : level_id * per_col]
            earlier = jnp.concatenate(forward_low, axis=0)
            partial_sum = jnp.einsum(
                "abpq,bqs->aps", panel, earlier, preferred_element_type=jnp.float32
            )
            row_total = lax.psum(partial_sum, "col")
            row_total = row_total.reshape((per_col, groups) + row_total.shape[1:])
            own_total = lax.dynamic_index_in_dim(
                row_total, my_col // row_count, axis=1, keepdims=False
            )
            solved = jnp.einsum(
                "mpq,mqs->mps",
                inverse_level,
                rhs_level - own_total,
                precision=lax.Precision.HIGHEST,
            )
            solved = spread(solved, "row", my_col % row_count)
        else:
            solved = jnp.einsum(
                "mpq,mqs->mps", inverse_level, rhs_level, precision=lax.Precision.HIGHEST
            )
        forward_vals.append(solved)
        forward_low.append(solved.astype(jnp.bfloat16))
    solution_parts = [None] * LEVELS
    later = []
    for level_id in reversed(range(LEVELS)):
        inverse_level = inverse_local[level_id * per_col : (level_id + 1) * per_col]
        resid = forward_vals[level_id]
        if level_id < LEVELS - 1:
            panel = masked[
                (level_id + 1) * per_row :, level_id * per_col : (level_id + 1) * per_col
            ]
            after = jnp.concatenate(later, axis=0)
            partial_sum = jnp.einsum(
                "abpq,aps->bqs", panel, after, preferred_element_type=jnp.float32
            )
            resid = resid - lax.psum(partial_sum, "row")
        solved = jnp.einsum("mqp,mqs->mps", inverse_level, resid, precision=lax.Precision.HIGHEST)
        solution_parts[level_id] = solved
        if level_id > 0:
            low_solved = solved.astype(jnp.bfloat16)
            pieces = lax.all_gather(low_solved[None], "col", axis=0, tiled=True)
            pieces = pieces.reshape((groups, row_count) + low_solved.shape)
            picked = lax.dynamic_index_in_dim(pieces, my_row, axis=1, keepdims=False)
            arranged = jnp.swapaxes(picked, 0, 1).reshape((per_row,) + low_solved.shape[1:])
            later = [arranged] + later
    solution = jnp.concatenate(solution_parts, axis=0)
    return solution[:, None]


def solution(mesh):
    in_specs = (
        P(None, "row", None, "col", None, None),
        P(None, "row", None, "col"),
        P(None, "col", None, None),
        P(None, "col", None, None),
    )
    out_specs = P(None, "col", None, None)
    return jax.shard_map(
        per_device, mesh=mesh, in_specs=in_specs, out_specs=out_specs, check_vma=False
    )
```

profile of v0, /device:TPU:2, one launch (start us, length us, event | category | flops | bytes accessed | tf_op | source)
XLA Modules:
  0.0 2246.1 jit_solution(3896068341786399089)
XLA Ops:
  8.5 7.4 bitcast_multiply_fusion
  17.9 116.1 %all-reduce.22.cloned.1.call-done = f32[4,128,256]{2,1,0:T(8,128)} async-done(((f32[4,128,256]{2,1,0:T(8,128)}), f32[4,128,256]{2,1,0:T(8,128)}) %all-reduce.22.cloned.1.call-update) | async-done | bytes 524304 | tf_op jit(solution)/shard_map/psum | solution.py:36
  135.9 72.4 %all-reduce.24.cloned.1.call-done = f32[1,128,256]{2,1,0:T(8,128)} async-done(((f32[1,128,256]{2,1,0:T(8,128)}), f32[1,128,256]{2,1,0:T(8,128)}) %all-reduce.24.cloned.1.call-update) | async-done | bytes 131088 | tf_op jit(solution)/shard_map/psum | solution.py:11
  209.3 2.0 convolution_bitcast_fusion.5
  211.3 111.8 %all-reduce.26.cloned.1.call-done = f32[4,128,256]{2,1,0:T(8,128)} async-done(((f32[4,128,256]{2,1,0:T(8,128)}), f32[4,128,256]{2,1,0:T(8,128)}) %all-reduce.26.cloned.1.call-update) | async-done | bytes 524304 | tf_op jit(solution)/shard_map/psum | solution.py:36
  325.1 72.3 %all-reduce.28.cloned.1.call-done = f32[1,128,256]{2,1,0:T(8,128)} async-done(((f32[1,128,256]{2,1,0:T(8,128)}), f32[1,128,256]{2,1,0:T(8,128)}) %all-reduce.28.cloned.1.call-update) | async-done | bytes 131088 | tf_op jit(solution)/shard_map/psum | solution.py:11
  398.3 2.1 convolution_bitcast_fusion.4
  400.5 111.6 %all-reduce.30.cloned.1.call-done = f32[4,128,256]{2,1,0:T(8,128)} async-done(((f32[4,128,256]{2,1,0:T(8,128)}), f32[4,128,256]{2,1,0:T(8,128)}) %all-reduce.30.cloned.1.call-update) | async-done | bytes 524304 | tf_op jit(solution)/shard_map/psum | solution.py:36
  514.0 72.3 %all-reduce.32.cloned.1.call-done = f32[1,128,256]{2,1,0:T(8,128)} async-done(((f32[1,128,256]{2,1,0:T(8,128)}), f32[1,128,256]{2,1,0:T(8,128)}) %all-reduce.32.cloned.1.call-update) | async-done | bytes 131088 | tf_op jit(solution)/shard_map/psum | solution.py:11
  587.3 2.1 convolution_bitcast_fusion.3
  589.5 111.6 %all-reduce.34.cloned.1.call-done = f32[4,128,256]{2,1,0:T(8,128)} async-done(((f32[4,128,256]{2,1,0:T(8,128)}), f32[4,128,256]{2,1,0:T(8,128)}) %all-reduce.34.cloned.1.call-update) | async-done | bytes 524304 | tf_op jit(solution)/shard_map/psum | solution.py:36
  703.1 72.4 %all-reduce.36.cloned.1.call-done = f32[1,128,256]{2,1,0:T(8,128)} async-done(((f32[1,128,256]{2,1,0:T(8,128)}), f32[1,128,256]{2,1,0:T(8,128)}) %all-reduce.36.cloned.1.call-update) | async-done | bytes 131088 | tf_op jit(solution)/shard_map/psum | solution.py:11
  776.4 2.3 convolution_bitcast_fusion.2
  778.8 111.6 %all-reduce.38.cloned.1.call-done = f32[4,128,256]{2,1,0:T(8,128)} async-done(((f32[4,128,256]{2,1,0:T(8,128)}), f32[4,128,256]{2,1,0:T(8,128)}) %all-reduce.38.cloned.1.call-update) | async-done | bytes 524304 | tf_op jit(solution)/shard_map/psum | solution.py:36
  892.3 72.3 %all-reduce.40.cloned.1.call-done = f32[1,128,256]{2,1,0:T(8,128)} async-done(((f32[1,128,256]{2,1,0:T(8,128)}), f32[1,128,256]{2,1,0:T(8,128)}) %all-reduce.40.cloned.1.call-update) | async-done | bytes 131088 | tf_op jit(solution)/shard_map/psum | solution.py:11
  965.6 2.3 convolution_bitcast_fusion.1
  967.9 111.7 %all-reduce.42.cloned.1.call-done = f32[4,128,256]{2,1,0:T(8,128)} async-done(((f32[4,128,256]{2,1,0:T(8,128)}), f32[4,128,256]{2,1,0:T(8,128)}) %all-reduce.42.cloned.1.call-update) | async-done | bytes 524304 | tf_op jit(solution)/shard_map/psum | solution.py:36
  1081.5 72.3 %all-reduce.44.cloned.1.call-done = f32[1,128,256]{2,1,0:T(8,128)} async-done(((f32[1,128,256]{2,1,0:T(8,128)}), f32[1,128,256]{2,1,0:T(8,128)}) %all-reduce.44.cloned.1.call-update) | async-done | bytes 131088 | tf_op jit(solution)/shard_map/psum | solution.py:11
  1154.8 2.4 convolution_bitcast_fusion
  1157.2 111.7 %all-reduce.46.cloned.1.call-done = f32[4,128,256]{2,1,0:T(8,128)} async-done(((f32[4,128,256]{2,1,0:T(8,128)}), f32[4,128,256]{2,1,0:T(8,128)}) %all-reduce.46.cloned.1.call-update) | async-done | bytes 524304 | tf_op jit(solution)/shard_map/psum | solution.py:36
  1270.8 72.3 %all-reduce.48.cloned.1.call-done = f32[128,256]{1,0:T(8,128)} async-done(((f32[128,256]{1,0:T(8,128)}), f32[128,256]{1,0:T(8,128)}) %all-reduce.48.cloned.1.call-update) | async-done | bytes 131088 | tf_op jit(solution)/shard_map/psum | solution.py:11
  1345.2 48.3 %all-gather.15.cloned.1.call-done = bf16[4096,256]{0,1:T(8,128)(2,1)} async-done(((bf16[128,256]{0,1:T(8,128)(2,1)}), bf16[4096,256]{0,1:T(8,128)(2,1)}) %all-gather.15.cloned.1.call-update) | async-done | bytes 2097168 | tf_op jit(solution)/shard_map/all_gather | solution.py:72
  1393.4 2.1 copy.59
  1398.4 71.8 %all-reduce.50.cloned.1.call-done = f32[1,128,256]{2,1,0:T(8,128)} async-done(((f32[1,128,256]{2,1,0:T(8,128)}), f32[1,128,256]{2,1,0:T(8,128)}) %all-reduce.50.cloned.1.call-update) | async-done | bytes 131088 | tf_op jit(solution)/shard_map/psum | solution.py:67
  1472.2 48.6 %all-gather.17.cloned.1.call-done = bf16[4096,256]{0,1:T(8,128)(2,1)} async-done(((bf16[128,256]{0,1:T(8,128)(2,1)}), bf16[4096,256]{0,1:T(8,128)(2,1)}) %all-gather.17.cloned.1.call-update) | async-done | bytes 2097168 | tf_op jit(solution)/shard_map/all_gather | solution.py:72
  1520.8 2.1 copy.60
  1525.9 71.8 %all-reduce.52.cloned.1.call-done = f32[1,128,256]{2,1,0:T(8,128)} async-done(((f32[1,128,256]{2,1,0:T(8,128)}), f32[1,128,256]{2,1,0:T(8,128)}) %all-reduce.52.cloned.1.call-update) | async-done | bytes 131088 | tf_op jit(solution)/shard_map/psum | solution.py:67
  1599.6 48.4 %all-gather.19.cloned.1.call-done = bf16[4096,256]{0,1:T(8,128)(2,1)} async-done(((bf16[128,256]{0,1:T(8,128)(2,1)}), bf16[4096,256]{0,1:T(8,128)(2,1)}) %all-gather.19.cloned.1.call-update) | async-done | bytes 2097168 | tf_op jit(solution)/shard_map/all_gather | solution.py:72
  1648.1 2.1 copy.61
  1651.2 2.0 convolution_bitcast_fusion.11
  1653.2 71.8 %all-reduce.54.cloned.1.call-done = f32[1,128,256]{2,1,0:T(8,128)} async-done(((f32[1,128,256]{2,1,0:T(8,128)}), f32[1,128,256]{2,1,0:T(8,128)}) %all-reduce.54.cloned.1.call-update) | async-done | bytes 131088 | tf_op jit(solution)/shard_map/psum | solution.py:67
  1727.2 48.6 %all-gather.21.cloned.1.call-done = bf16[4096,256]{0,1:T(8,128)(2,1)} async-done(((bf16[128,256]{0,1:T(8,128)(2,1)}), bf16[4096,256]{0,1:T(8,128)(2,1)}) %all-gather.21.cloned.1.call-update) | async-done | bytes 2097168 | tf_op jit(solution)/shard_map/all_gather | solution.py:72
  1775.8 2.1 copy.62
  1778.9 2.1 convolution_bitcast_fusion.13
  1781.1 71.8 %all-reduce.56.cloned.1.call-done = f32[1,128,256]{2,1,0:T(8,128)} async-done(((f32[1,128,256]{2,1,0:T(8,128)}), f32[1,128,256]{2,1,0:T(8,128)}) %all-reduce.56.cloned.1.call-update) | async-done | bytes 131088 | tf_op jit(solution)/shard_map/psum | solution.py:67
  1854.9 48.4 %all-gather.23.cloned.1.call-done = bf16[4096,256]{0,1:T(8,128)(2,1)} async-done(((bf16[128,256]{0,1:T(8,128)(2,1)}), bf16[4096,256]{0,1:T(8,128)(2,1)}) %all-gather.23.cloned.1.call-update) | async-done | bytes 2097168 | tf_op jit(solution)/shard_map/all_gather | solution.py:72
  1903.3 2.1 copy.63
  1906.5 2.1 convolution_bitcast_fusion.12
  1908.8 71.8 %all-reduce.58.cloned.1.call-done = f32[1,128,256]{2,1,0:T(8,128)} async-done(((f32[1,128,256]{2,1,0:T(8,128)}), f32[1,128,256]{2,1,0:T(8,128)}) %all-reduce.58.cloned.1.call-update) | async-done | bytes 131088 | tf_op jit(solution)/shard_map/psum | solution.py:67
  1980.5 2.0 bitcast_convert_fusion.1
  1982.6 48.7 %all-gather.25.cloned.1.call-done = bf16[4096,256]{0,1:T(8,128)(2,1)} async-done(((bf16[128,256]{0,1:T(8,128)(2,1)}), bf16[4096,256]{0,1:T(8,128)(2,1)}) %all-gather.25.cloned.1.call-update) | async-done | bytes 2097168 | tf_op jit(solution)/shard_map/all_gather | solution.py:72
  2031.3 2.1 copy.64
  2034.5 2.2 convolution_bitcast_fusion.7
  2036.8 71.8 %all-reduce.60.cloned.1.call-done = f32[1,128,256]{2,1,0:T(8,128)} async-done(((f32[1,128,256]{2,1,0:T(8,128)}), f32[1,128,256]{2,1,0:T(8,128)}) %all-reduce.60.cloned.1.call-update) | async-done | bytes 131088 | tf_op jit(solution)/shard_map/psum | solution.py:67
  2110.7 48.2 %all-gather.27.cloned.1.call-done = bf16[4096,256]{0,1:T(8,128)(2,1)} async-done(((bf16[128,256]{0,1:T(8,128)(2,1)}), bf16[4096,256]{0,1:T(8,128)(2,1)}) %all-gather.27.cloned.1.call-update) | async-done | bytes 2097168 | tf_op jit(solution)/shard_map/all_gather | solution.py:72
  2158.9 2.1 copy.65
  2162.2 2.4 convolution_bitcast_fusion.6
  2164.6 71.8 %all-reduce.62.cloned.1.call-done = f32[1,128,256]{2,1,0:T(8,128)} async-done(((f32[1,128,256]{2,1,0:T(8,128)}), f32[1,128,256]{2,1,0:T(8,128)}) %all-reduce.62.cloned.1.call-update) | async-done | bytes 131088 | tf_op jit(solution)/shard_map/psum | solution.py:67
  (149 shorter events, 49.5 us)
Async XLA Ops:
  6.5 127.4 %all-reduce.22.cloned.1.call-start = ((), (), s32[]{:S(2)}) async-start(), calls=%async_computation | async-start | bytes 1048576 | tf_op jit(solution)/shard_map/psum | solution.py:36
  8.4 125.5 %copy-start = (f32[8,1,128,128]{3,2,1,0:T(8,128)S(1)}, f32[8,1,128,128]{3,2,1,0:T(8,128)}, u32[]{:S(2)}) copy-start(f32[8,1,128,128]{3,2,1,0:T(8,128)} %param.7) | copy-start | bytes 1572868
  8.5 125.5 %copy-start.1 = (f32[8,1,128,256]{3,2,1,0:T(8,128)S(1)}, f32[8,1,128,256]{3,2,1,0:T(8,128)}, u32[]{:S(2)}) copy-start(f32[8,1,128,256]{3,2,1,0:T(8,128)} %param.6) | copy-start | bytes 3145732
  17.8 190.6 %all-reduce.24.cloned.1.call-start = ((), (), s32[]{:S(2)}) async-start(), calls=%async_computation.1 | async-start | bytes 262144 | tf_op jit(solution)/shard_map/psum | solution.py:11
  135.8 187.3 %all-reduce.26.cloned.1.call-start = ((), (), s32[]{:S(2)}) async-start(), calls=%async_computation.2 | async-start | bytes 1048576 | tf_op jit(solution)/shard_map/psum | solution.py:36
  211.3 186.1 %all-reduce.28.cloned.1.call-start = ((), (), s32[]{:S(2)}) async-start(), calls=%async_computation.3 | async-start | bytes 262144 | tf_op jit(solution)/shard_map/psum | solution.py:11
  325.0 187.1 %all-reduce.30.cloned.1.call-start = ((), (), s32[]{:S(2)}) async-start(), calls=%async_computation.4 | async-start | bytes 1048576 | tf_op jit(solution)/shard_map/psum | solution.py:36
  400.4 185.9 %all-reduce.32.cloned.1.call-start = ((), (), s32[]{:S(2)}) async-start(), calls=%async_computation.5 | async-start | bytes 262144 | tf_op jit(solution)/shard_map/psum | solution.py:11
  514.0 187.1 %all-reduce.34.cloned.1.call-start = ((), (), s32[]{:S(2)}) async-start(), calls=%async_computation.6 | async-start | bytes 1048576 | tf_op jit(solution)/shard_map/psum | solution.py:36
  589.4 186.1 %all-reduce.36.cloned.1.call-start = ((), (), s32[]{:S(2)}) async-start(), calls=%async_computation.7 | async-start | bytes 262144 | tf_op jit(solution)/shard_map/psum | solution.py:11
  703.0 187.4 %all-reduce.38.cloned.1.call-start = ((), (), s32[]{:S(2)}) async-start(), calls=%async_computation.8 | async-start | bytes 1048576 | tf_op jit(solution)/shard_map/psum | solution.py:36
  778.7 185.9 %all-reduce.40.cloned.1.call-start = ((), (), s32[]{:S(2)}) async-start(), calls=%async_computation.9 | async-start | bytes 262144 | tf_op jit(solution)/shard_map/psum | solution.py:11
  892.3 187.3 %all-reduce.42.cloned.1.call-start = ((), (), s32[]{:S(2)}) async-start(), calls=%async_computation.10 | async-start | bytes 1048576 | tf_op jit(solution)/shard_map/psum | solution.py:36
  967.9 186.0 %all-reduce.44.cloned.1.call-start = ((), (), s32[]{:S(2)}) async-start(), calls=%async_computation.11 | async-start | bytes 262144 | tf_op jit(solution)/shard_map/psum | solution.py:11
  1081.5 187.4 %all-reduce.46.cloned.1.call-start = ((), (), s32[]{:S(2)}) async-start(), calls=%async_computation.12 | async-start | bytes 1048576 | tf_op jit(solution)/shard_map/psum | solution.py:36
  1157.2 186.0 %all-reduce.48.cloned.1.call-start = ((), (), s32[]{:S(2)}) async-start(), calls=%async_computation.13 | async-start | bytes 262144 | tf_op jit(solution)/shard_map/psum | solution.py:11
  1270.8 122.7 %all-gather.15.cloned.1.call-start = ((), (), s32[]{:S(2)}) async-start(), calls=%async_computation.21 | async-start | bytes 2162688 | tf_op jit(solution)/shard_map/all_gather | solution.py:72
  1345.1 125.1 %all-reduce.50.cloned.1.call-start = ((), (), s32[]{:S(2)}) async-start(), calls=%async_computation.14 | async-start | bytes 262144 | tf_op jit(solution)/shard_map/psum | solution.py:67
  1395.5 74.7 %copy-start.9 = (f32[1,128,256]{2,1,0:T(8,128)S(1)}, f32[1,128,256]{2,1,0:T(8,128)}, u32[]{:S(2)}) copy-start(f32[1,128,256]{2,1,0:T(8,128)} %all-reduce.44.cloned.1.call-done) | copy-start | bytes 393220
  1398.4 122.4 %all-gather.17.cloned.1.call-start = ((), (), s32[]{:S(2)}) async-start(), calls=%async_computation.22 | async-start | bytes 2162688 | tf_op jit(solution)/shard_map/all_gather | solution.py:72
  1472.1 125.5 %all-reduce.52.cloned.1.call-start = ((), (), s32[]{:S(2)}) async-start(), calls=%async_computation.15 | async-start | bytes 262144 | tf_op jit(solution)/shard_map/psum | solution.py:67
  1522.9 74.8 %copy-start.6 = (f32[1,128,256]{2,1,0:T(8,128)S(1)}, f32[1,128,256]{2,1,0:T(8,128)}, u32[]{:S(2)}) copy-start(f32[1,128,256]{2,1,0:T(8,128)} %all-reduce.40.cloned.1.call-done) | copy-start | bytes 393220
  1525.8 122.3 %all-gather.19.cloned.1.call-start = ((), (), s32[]{:S(2)}) async-start(), calls=%async_computation.23 | async-start | bytes 2162688 | tf_op jit(solution)/shard_map/all_gather | solution.py:72
  1599.6 125.4 %all-reduce.54.cloned.1.call-start = ((), (), s32[]{:S(2)}) async-start(), calls=%async_computation.16 | async-start | bytes 262144 | tf_op jit(solution)/shard_map/psum | solution.py:67
  1650.7 74.3 %copy-start.5 = (f32[1,128,256]{2,1,0:T(8,128)S(1)}, f32[1,128,256]{2,1,0:T(8,128)}, u32[]{:S(2)}) copy-start(f32[1,128,256]{2,1,0:T(8,128)} %all-reduce.36.cloned.1.call-done) | copy-start | bytes 393220
  1653.2 122.6 %all-gather.21.cloned.1.call-start = ((), (), s32[]{:S(2)}) async-start(), calls=%async_computation.24 | async-start | bytes 2162688 | tf_op jit(solution)/shard_map/all_gather | solution.py:72
  1727.0 125.9 %all-reduce.56.cloned.1.call-start = ((), (), s32[]{:S(2)}) async-start(), calls=%async_computation.17 | async-start | bytes 262144 | tf_op jit(solution)/shard_map/psum | solution.py:67
  1778.9 74.0 %copy-start.4 = (f32[1,128,256]{2,1,0:T(8,128)S(1)}, f32[1,128,256]{2,1,0:T(8,128)}, u32[]{:S(2)}) copy-start(f32[1,128,256]{2,1,0:T(8,128)} %all-reduce.32.cloned.1.call-done) | copy-start | bytes 393220
  1781.0 122.3 %all-gather.23.cloned.1.call-start = ((), (), s32[]{:S(2)}) async-start(), calls=%async_computation.25 | async-start | bytes 2162688 | tf_op jit(solution)/shard_map/all_gather | solution.py:72
  1854.8 125.7 %all-reduce.58.cloned.1.call-start = ((), (), s32[]{:S(2)}) async-start(), calls=%async_computation.18 | async-start | bytes 262144 | tf_op jit(solution)/shard_map/psum | solution.py:67
  1906.5 74.1 %copy-start.3 = (f32[1,128,256]{2,1,0:T(8,128)S(1)}, f32[1,128,256]{2,1,0:T(8,128)}, u32[]{:S(2)}) copy-start(f32[1,128,256]{2,1,0:T(8,128)} %all-reduce.28.cloned.1.call-done) | copy-start | bytes 393220
  1908.7 122.6 %all-gather.25.cloned.1.call-start = ((), (), s32[]{:S(2)}) async-start(), calls=%async_computation.26 | async-start | bytes 2162688 | tf_op jit(solution)/shard_map/all_gather | solution.py:72
  1982.5 126.1 %all-reduce.60.cloned.1.call-start = ((), (), s32[]{:S(2)}) async-start(), calls=%async_computation.19 | async-start | bytes 262144 | tf_op jit(solution)/shard_map/psum | solution.py:67
  2034.5 74.1 %copy-start.2 = (f32[1,128,256]{2,1,0:T(8,128)S(1)}, f32[1,128,256]{2,1,0:T(8,128)}, u32[]{:S(2)}) copy-start(f32[1,128,256]{2,1,0:T(8,128)} %all-reduce.24.cloned.1.call-done) | copy-start | bytes 393220
  2036.8 122.1 %all-gather.27.cloned.1.call-start = ((), (), s32[]{:S(2)}) async-start(), calls=%async_computation.27 | async-start | bytes 2162688 | tf_op jit(solution)/shard_map/all_gather | solution.py:72
  2110.6 125.8 %all-reduce.62.cloned.1.call-start = ((), (), s32[]{:S(2)}) async-start(), calls=%async_computation.20 | async-start | bytes 262144 | tf_op jit(solution)/shard_map/psum | solution.py:67
  2162.2 75.5 %copy-start.10 = (f32[256,128]{1,0:T(8,128)S(1)}, f32[256,128]{1,0:T(8,128)}, u32[]{:S(2)}) copy-start(f32[256,128]{1,0:T(8,128)} %get-tuple-element.39) | copy-start | bytes 393220
  2162.2 75.6 %copy-start.8 = (f32[256,128]{1,0:T(8,128)S(1)}, f32[256,128]{1,0:T(8,128)}, u32[]{:S(2)}) copy-start(f32[256,128]{1,0:T(8,128)} %get-tuple-element.37) | copy-start | bytes 393220
  2162.2 75.6 %copy-start.7 = (f32[256,128]{1,0:T(8,128)S(1)}, f32[256,128]{1,0:T(8,128)}, u32[]{:S(2)}) copy-start(f32[256,128]{1,0:T(8,128)} %get-tuple-element.35) | copy-start | bytes 393220
Sparse Core Ops, SparseCore 0:
  17.9 116.0 all-reduce.21
  136.4 71.9 all-reduce.23
  211.6 111.5 all-reduce.25
  325.4 71.9 all-reduce.27
  400.5 111.5 all-reduce.29
  514.4 71.9 all-reduce.31
  589.5 111.5 all-reduce.33
  703.5 71.9 all-reduce.35
  778.8 111.5 all-reduce.37
  892.7 71.9 all-reduce.39
  968.0 111.5 all-reduce.41
  1081.9 71.9 all-reduce.43
  1157.3 111.5 all-reduce.45
  1271.2 71.9 all-reduce.47
  1345.5 47.9 all-gather.14
  1398.5 71.6 all-reduce.49
  1472.8 47.9 all-gather.16
  1525.9 71.6 all-reduce.51
  1600.1 47.9 all-gather.18
  1653.3 71.6 all-reduce.53
  1727.8 47.9 all-gather.20
  1781.1 71.6 all-reduce.55
  1855.3 47.9 all-gather.22
  1908.8 71.6 all-reduce.57
  1983.3 47.9 all-gather.24
  2036.9 71.6 all-reduce.59
  2110.9 47.9 all-gather.26
  2164.7 71.6 all-reduce.61
where the time goes:
time: 2250 us
  waiting for transfers between devices  2130 us (95%)
  matrix products  58.4 us (3%)
  local copies, waits for them, and re-layouts  23.5 us (1%)
    psum x7, waiting for transfers between devices, per_device(): row_total = lax.psum(partial_sum, 'col')  786 us
    psum x7, waiting for transfers between devices, spread(): return lax.psum(kept, axis)  507 us
    psum x7, waiting for transfers between devices, per_device(): resid = resid - lax.psum(partial_sum, 'row')  502 us
    all_gather x7, waiting for transfers between devices, per_device(): pieces = lax.all_gather(low_solved[None], 'col', axis=0, tiled=True)  339 us
  transfers between devices with their start and end apart: 28, of which 28 were waited for; matrix products, arithmetic and copies ran while one was open for 0% of the time, Pallas kernels for 0%

commit v1 on v0

--- a/solution.py
+++ b/solution.py
@@ -33,7 +33,11 @@
             partial_sum = jnp.einsum(
                 "abpq,bqs->aps", panel, earlier, preferred_element_type=jnp.float32
             )
-            row_total = lax.psum(partial_sum, "col")
+            row_total = partial_sum
+            for hop in (1, 2, 4, 8, 16):
+                row_total = row_total + lax.ppermute(
+                    row_total, "col", [(dev, dev ^ hop) for dev in range(32)]
+                )
             row_total = row_total.reshape((per_col, groups) + row_total.shape[1:])
             own_total = lax.dynamic_index_in_dim(
                 row_total, my_col // row_count, axis=1, keepdims=False

time: 2250 us -> 1840 us (0.82)
  waiting for transfers between devices: 2130 us -> 1680 us
  starting transfers between devices: 1.32 us -> 54.2 us
    psum x7 -> x0, waiting for transfers between devices: 786 us -> none  [per_device(): row_total = lax.psum(partial_sum, 'col')]
    ppermute x0 -> x35, waiting for transfers between devices: none -> 343 us  [per_device(): lax.ppermute(row_total, 'col', [(dev, dev ^ hop) for dev in range(32)])]
    ppermute x0 -> x35, starting transfers between devices: none -> 53.1 us  [per_device(): lax.ppermute(row_total, 'col', [(dev, dev ^ hop) for dev in range(32)])]
  transfers between devices with their start and end apart: 28 -> 56, of which waited for: 28 -> 56; matrix products, arithmetic and copies ran while one was open for 0% -> 0% of each run, Pallas kernels for 0% -> 0%
where the time goes in v1:
time: 1840 us; the launch traced here: 1830 us
  waiting for transfers between devices  1680 us (91%)
  starting transfers between devices  54.2 us (3%)
  matrix products  46.7 us (3%)
  local copies, waits for them, and re-layouts  23.5 us (1%)
    psum x7, waiting for transfers between devices, per_device(): resid = resid - lax.psum(partial_sum, 'row')  502 us
    psum x7, waiting for transfers between devices, spread(): return lax.psum(kept, axis)  493 us
    ppermute x35, waiting for transfers between devices, per_device(): lax.ppermute(row_total, 'col', [(dev, dev ^ hop) for dev in range(32)])  343 us
    all_gather x7, waiting for transfers between devices, per_device(): pieces = lax.all_gather(low_solved[None], 'col', axis=0, tiled=True)  339 us
    ppermute x35, starting transfers between devices, per_device(): lax.ppermute(row_total, 'col', [(dev, dev ^ hop) for dev in range(32)])  53.1 us
  transfers between devices with their start and end apart: 56, of which 56 were waited for; matrix products, arithmetic and copies ran while one was open for 0% of the time, Pallas kernels for 0%

profile of v1, /device:TPU:2, one launch (start us, length us, event | category | flops | bytes accessed | tf_op | source)
XLA Modules:
  0.0 1832.8 jit_solution(3501886412860637948)
XLA Ops:
  21.3 12.2 collective-permute-done.1
  35.3 13.4 collective-permute-done.2
  49.6 11.8 collective-permute-done.3
  63.6 11.1 collective-permute-done.4
  75.7 73.4 %all-reduce.15.cloned.1.call-done = f32[1,128,256]{2,1,0:T(8,128)} async-done(((f32[1,128,256]{2,1,0:T(8,128)}), f32[1,128,256]{2,1,0:T(8,128)}) %all-reduce.15.cloned.1.call-update) | async-done | bytes 131088 | tf_op jit(solution)/shard_map/psum | solution.py:11
  153.9 13.4 collective-permute-done.6
  169.6 12.6 collective-permute-done.7
  183.8 10.7 collective-permute-done.8
  197.7 10.2 collective-permute-done.9
  208.9 69.9 %all-reduce.17.cloned.1.call-done = f32[1,128,256]{2,1,0:T(8,128)} async-done(((f32[1,128,256]{2,1,0:T(8,128)}), f32[1,128,256]{2,1,0:T(8,128)}) %all-reduce.17.cloned.1.call-update) | async-done | bytes 131088 | tf_op jit(solution)/shard_map/psum | solution.py:11
  283.8 13.4 collective-permute-done.11
  299.4 12.6 collective-permute-done.12
  313.7 10.7 collective-permute-done.13
  327.6 10.2 collective-permute-done.14
  338.8 70.0 %all-reduce.19.cloned.1.call-done = f32[1,128,256]{2,1,0:T(8,128)} async-done(((f32[1,128,256]{2,1,0:T(8,128)}), f32[1,128,256]{2,1,0:T(8,128)}) %all-reduce.19.cloned.1.call-update) | async-done | bytes 131088 | tf_op jit(solution)/shard_map/psum | solution.py:11
  414.3 13.4 collective-permute-done.16
  429.9 12.6 collective-permute-done.17
  444.1 10.7 collective-permute-done.18
  469.3 69.9 %all-reduce.21.cloned.1.call-done = f32[1,128,256]{2,1,0:T(8,128)} async-done(((f32[1,128,256]{2,1,0:T(8,128)}), f32[1,128,256]{2,1,0:T(8,128)}) %all-reduce.21.cloned.1.call-update) | async-done | bytes 131088 | tf_op jit(solution)/shard_map/psum | solution.py:11
  544.3 13.4 collective-permute-done.21
  559.9 12.6 collective-permute-done.22
  574.2 10.7 collective-permute-done.23
  588.1 10.2 collective-permute-done.24
  599.3 69.9 %all-reduce.23.cloned.1.call-done = f32[1,128,256]{2,1,0:T(8,128)} async-done(((f32[1,128,256]{2,1,0:T(8,128)}), f32[1,128,256]{2,1,0:T(8,128)}) %all-reduce.23.cloned.1.call-update) | async-done | bytes 131088 | tf_op jit(solution)/shard_map/psum | solution.py:11
  674.4 13.4 collective-permute-done.26
  690.1 12.6 collective-permute-done.27
  704.3 10.7 collective-permute-done.28
  718.2 10.2 collective-permute-done.29
  729.4 70.0 %all-reduce.25.cloned.1.call-done = f32[1,128,256]{2,1,0:T(8,128)} async-done(((f32[1,128,256]{2,1,0:T(8,128)}), f32[1,128,256]{2,1,0:T(8,128)}) %all-reduce.25.cloned.1.call-update) | async-done | bytes 131088 | tf_op jit(solution)/shard_map/psum | solution.py:11
  804.7 13.4 collective-permute-done.31
  820.5 12.6 collective-permute-done.32
  834.7 10.7 collective-permute-done.33
  848.6 10.2 collective-permute-done.34
  859.9 69.9 %all-reduce.27.cloned.1.call-done = f32[128,256]{1,0:T(8,128)} async-done(((f32[128,256]{1,0:T(8,128)}), f32[128,256]{1,0:T(8,128)}) %all-reduce.27.cloned.1.call-update) | async-done | bytes 131088 | tf_op jit(solution)/shard_map/psum | solution.py:11
  931.8 48.7 %all-gather.15.cloned.1.call-done = bf16[4096,256]{0,1:T(8,128)(2,1)} async-done(((bf16[128,256]{0,1:T(8,128)(2,1)}), bf16[4096,256]{0,1:T(8,128)(2,1)}) %all-gather.15.cloned.1.call-update) | async-done | bytes 2097168 | tf_op jit(solution)/shard_map/all_gather | solution.py:76
  985.5 71.8 %all-reduce.29.cloned.1.call-done = f32[1,128,256]{2,1,0:T(8,128)} async-done(((f32[1,128,256]{2,1,0:T(8,128)}), f32[1,128,256]{2,1,0:T(8,128)}) %all-reduce.29.cloned.1.call-update) | async-done | bytes 131088 | tf_op jit(solution)/shard_map/psum | solution.py:71
  1059.3 48.3 %all-gather.17.cloned.1.call-done = bf16[4096,256]{0,1:T(8,128)(2,1)} async-done(((bf16[128,256]{0,1:T(8,128)(2,1)}), bf16[4096,256]{0,1:T(8,128)(2,1)}) %all-gather.17.cloned.1.call-update) | async-done | bytes 2097168 | tf_op jit(solution)/shard_map/all_gather | solution.py:76
  1112.6 71.8 %all-reduce.31.cloned.1.call-done = f32[1,128,256]{2,1,0:T(8,128)} async-done(((f32[1,128,256]{2,1,0:T(8,128)}), f32[1,128,256]{2,1,0:T(8,128)}) %all-reduce.31.cloned.1.call-update) | async-done | bytes 131088 | tf_op jit(solution)/shard_map/psum | solution.py:71
  1186.4 48.6 %all-gather.19.cloned.1.call-done = bf16[4096,256]{0,1:T(8,128)(2,1)} async-done(((bf16[128,256]{0,1:T(8,128)(2,1)}), bf16[4096,256]{0,1:T(8,128)(2,1)}) %all-gather.19.cloned.1.call-update) | async-done | bytes 2097168 | tf_op jit(solution)/shard_map/all_gather | solution.py:76
  1240.2 71.8 %all-reduce.33.cloned.1.call-done = f32[1,128,256]{2,1,0:T(8,128)} async-done(((f32[1,128,256]{2,1,0:T(8,128)}), f32[1,128,256]{2,1,0:T(8,128)}) %all-reduce.33.cloned.1.call-update) | async-done | bytes 131088 | tf_op jit(solution)/shard_map/psum | solution.py:71
  1313.9 48.3 %all-gather.21.cloned.1.call-done = bf16[4096,256]{0,1:T(8,128)(2,1)} async-done(((bf16[128,256]{0,1:T(8,128)(2,1)}), bf16[4096,256]{0,1:T(8,128)(2,1)}) %all-gather.21.cloned.1.call-update) | async-done | bytes 2097168 | tf_op jit(solution)/shard_map/all_gather | solution.py:76
  1367.6 71.8 %all-reduce.35.cloned.1.call-done = f32[1,128,256]{2,1,0:T(8,128)} async-done(((f32[1,128,256]{2,1,0:T(8,128)}), f32[1,128,256]{2,1,0:T(8,128)}) %all-reduce.35.cloned.1.call-update) | async-done | bytes 131088 | tf_op jit(solution)/shard_map/psum | solution.py:71
  1441.4 48.6 %all-gather.23.cloned.1.call-done = bf16[4096,256]{0,1:T(8,128)(2,1)} async-done(((bf16[128,256]{0,1:T(8,128)(2,1)}), bf16[4096,256]{0,1:T(8,128)(2,1)}) %all-gather.23.cloned.1.call-update) | async-done | bytes 2097168 | tf_op jit(solution)/shard_map/all_gather | solution.py:76
  1495.4 71.8 %all-reduce.37.cloned.1.call-done = f32[1,128,256]{2,1,0:T(8,128)} async-done(((f32[1,128,256]{2,1,0:T(8,128)}), f32[1,128,256]{2,1,0:T(8,128)}) %all-reduce.37.cloned.1.call-update) | async-done | bytes 131088 | tf_op jit(solution)/shard_map/psum | solution.py:71
  1569.4 48.0 %all-gather.25.cloned.1.call-done = bf16[4096,256]{0,1:T(8,128)(2,1)} async-done(((bf16[128,256]{0,1:T(8,128)(2,1)}), bf16[4096,256]{0,1:T(8,128)(2,1)}) %all-gather.25.cloned.1.call-update) | async-done | bytes 2097168 | tf_op jit(solution)/shard_map/all_gather | solution.py:76
  1623.1 71.8 %all-reduce.39.cloned.1.call-done = f32[1,128,256]{2,1,0:T(8,128)} async-done(((f32[1,128,256]{2,1,0:T(8,128)}), f32[1,128,256]{2,1,0:T(8,128)}) %all-reduce.39.cloned.1.call-update) | async-done | bytes 131088 | tf_op jit(solution)/shard_map/psum | solution.py:71
  1696.9 48.5 %all-gather.27.cloned.1.call-done = bf16[4096,256]{0,1:T(8,128)(2,1)} async-done(((bf16[128,256]{0,1:T(8,128)(2,1)}), bf16[4096,256]{0,1:T(8,128)(2,1)}) %all-gather.27.cloned.1.call-update) | async-done | bytes 2097168 | tf_op jit(solution)/shard_map/all_gather | solution.py:76
  1751.1 71.8 %all-reduce.41.cloned.1.call-done = f32[1,128,256]{2,1,0:T(8,128)} async-done(((f32[1,128,256]{2,1,0:T(8,128)}), f32[1,128,256]{2,1,0:T(8,128)}) %all-reduce.41.cloned.1.call-update) | async-done | bytes 131088 | tf_op jit(solution)/shard_map/psum | solution.py:71
  (226 shorter events, 163.5 us)
Async XLA Ops:
  6.5 142.6 %all-reduce.15.cloned.1.call-start = ((), (), s32[]{:S(2)}) async-start(), calls=%async_computation | async-start | bytes 262144 | tf_op jit(solution)/shard_map/psum | solution.py:11
  19.0 14.6 collective-permute-start.1
  33.6 15.0 collective-permute-start.2
  48.8 12.6 collective-permute-start.3
  61.5 13.2 collective-permute-start.4
  75.7 203.2 %all-reduce.17.cloned.1.call-start = ((), (), s32[]{:S(2)}) async-start(), calls=%async_computation.1 | async-start | bytes 262144 | tf_op jit(solution)/shard_map/psum | solution.py:11
  153.3 14.1 collective-permute-start.6
  167.4 14.7 collective-permute-start.7
  182.2 12.3 collective-permute-start.8
  194.6 13.3 collective-permute-start.9
  208.9 199.9 %all-reduce.19.cloned.1.call-start = ((), (), s32[]{:S(2)}) async-start(), calls=%async_computation.2 | async-start | bytes 262144 | tf_op jit(solution)/shard_map/psum | solution.py:11
  283.2 14.1 collective-permute-start.11
  297.3 14.7 collective-permute-start.12
  312.1 12.3 collective-permute-start.13
  324.5 13.3 collective-permute-start.14
  338.8 200.4 %all-reduce.21.cloned.1.call-start = ((), (), s32[]{:S(2)}) async-start(), calls=%async_computation.3 | async-start | bytes 262144 | tf_op jit(solution)/shard_map/psum | solution.py:11
  413.6 14.1 collective-permute-start.16
  427.7 14.7 collective-permute-start.17
  442.5 12.3 collective-permute-start.18
  454.9 13.3 collective-permute-start.19
  469.2 200.0 %all-reduce.23.cloned.1.call-start = ((), (), s32[]{:S(2)}) async-start(), calls=%async_computation.4 | async-start | bytes 262144 | tf_op jit(solution)/shard_map/psum | solution.py:11
  543.7 14.1 collective-permute-start.21
  557.8 14.7 collective-permute-start.22
  572.6 12.3 collective-permute-start.23
  585.0 13.3 collective-permute-start.24
  599.3 200.2 %all-reduce.25.cloned.1.call-start = ((), (), s32[]{:S(2)}) async-start(), calls=%async_computation.5 | async-start | bytes 262144 | tf_op jit(solution)/shard_map/psum | solution.py:11
  673.8 14.1 collective-permute-start.26
  687.9 14.7 collective-permute-start.27
  715.1 13.3 collective-permute-start.29
  729.4 200.4 %all-reduce.27.cloned.1.call-start = ((), (), s32[]{:S(2)}) async-start(), calls=%async_computation.6 | async-start | bytes 262144 | tf_op jit(solution)/shard_map/psum | solution.py:11
  804.0 14.1 collective-permute-start.31
  818.2 14.9 collective-permute-start.32
  833.1 12.3 collective-permute-start.33
  845.5 13.3 collective-permute-start.34
  859.8 120.7 %all-gather.15.cloned.1.call-start = ((), (), s32[]{:S(2)}) async-start(), calls=%async_computation.14 | async-start | bytes 2162688 | tf_op jit(solution)/shard_map/all_gather | solution.py:76
  931.7 125.6 %all-reduce.29.cloned.1.call-start = ((), (), s32[]{:S(2)}) async-start(), calls=%async_computation.7 | async-start | bytes 262144 | tf_op jit(solution)/shard_map/psum | solution.py:71
  985.5 122.1 %all-gather.17.cloned.1.call-start = ((), (), s32[]{:S(2)}) async-start(), calls=%async_computation.15 | async-start | bytes 2162688 | tf_op jit(solution)/shard_map/all_gather | solution.py:76
  1059.2 125.2 %all-reduce.31.cloned.1.call-start = ((), (), s32[]{:S(2)}) async-start(), calls=%async_computation.8 | async-start | bytes 262144 | tf_op jit(solution)/shard_map/psum | solution.py:71
  1112.6 122.4 %all-gather.19.cloned.1.call-start = ((), (), s32[]{:S(2)}) async-start(), calls=%async_computation.16 | async-start | bytes 2162688 | tf_op jit(solution)/shard_map/all_gather | solution.py:76
  1186.4 125.6 %all-reduce.33.cloned.1.call-start = ((), (), s32[]{:S(2)}) async-start(), calls=%async_computation.9 | async-start | bytes 262144 | tf_op jit(solution)/shard_map/psum | solution.py:71
  1240.1 122.1 %all-gather.21.cloned.1.call-start = ((), (), s32[]{:S(2)}) async-start(), calls=%async_computation.17 | async-start | bytes 2162688 | tf_op jit(solution)/shard_map/all_gather | solution.py:76
  1313.9 125.4 %all-reduce.35.cloned.1.call-start = ((), (), s32[]{:S(2)}) async-start(), calls=%async_computation.10 | async-start | bytes 262144 | tf_op jit(solution)/shard_map/psum | solution.py:71
  1367.5 122.4 %all-gather.23.cloned.1.call-start = ((), (), s32[]{:S(2)}) async-start(), calls=%async_computation.18 | async-start | bytes 2162688 | tf_op jit(solution)/shard_map/all_gather | solution.py:76
  1441.3 125.9 %all-reduce.37.cloned.1.call-start = ((), (), s32[]{:S(2)}) async-start(), calls=%async_computation.11 | async-start | bytes 262144 | tf_op jit(solution)/shard_map/psum | solution.py:71
  1495.3 122.1 %all-gather.25.cloned.1.call-start = ((), (), s32[]{:S(2)}) async-start(), calls=%async_computation.19 | async-start | bytes 2162688 | tf_op jit(solution)/shard_map/all_gather | solution.py:76
  1569.2 125.7 %all-reduce.39.cloned.1.call-start = ((), (), s32[]{:S(2)}) async-start(), calls=%async_computation.12 | async-start | bytes 262144 | tf_op jit(solution)/shard_map/psum | solution.py:71
  1623.0 122.4 %all-gather.27.cloned.1.call-start = ((), (), s32[]{:S(2)}) async-start(), calls=%async_computation.20 | async-start | bytes 2162688 | tf_op jit(solution)/shard_map/all_gather | solution.py:76
  1696.8 126.1 %all-reduce.41.cloned.1.call-start = ((), (), s32[]{:S(2)}) async-start(), calls=%async_computation.13 | async-start | bytes 262144 | tf_op jit(solution)/shard_map/psum | solution.py:71
  (19 other events, 781.6 us)
Sparse Core Ops, SparseCore 0:
  75.8 73.2 all-reduce.14
  209.0 69.8 all-reduce.16
  338.9 69.8 all-reduce.18
  469.3 69.8 all-reduce.20
  599.4 69.8 all-reduce.22
  729.5 69.8 all-reduce.24
  859.9 69.8 all-reduce.26
  932.6 47.9 all-gather.14
  985.6 71.6 all-reduce.28
  1059.6 47.9 all-gather.16
  1112.7 71.6 all-reduce.30
  1187.0 47.9 all-gather.18
  1240.2 71.6 all-reduce.32
  1314.3 47.9 all-gather.20
  1367.6 71.6 all-reduce.34
  1442.0 47.9 all-gather.22
  1495.5 71.6 all-reduce.36
  1569.5 47.9 all-gather.24
  1623.1 71.6 all-reduce.38
  1697.4 47.9 all-gather.26
  1751.3 71.6 all-reduce.40
